TPU v7x, 32 devices: a whole 2x2x4 slice. The times are simulated.
32 devices in a mesh: dp: 4 (over y, x), space: 8 (over z, core).
Axes of the slice: x: 2, y: 2, z: 4, core: 2. Of those that a mesh axis runs over, the one named last changes fastest.
Arguments:
- features: bfloat16 [4, 2048, 256], P('dp', 'space'), may hold values from -6 to 6
- neighbours: int32 [4, 27, 2048], P('dp', None, 'space'), may hold values from -1 to 2047, as said below
- parents: int32 [4, 2048], P('dp', 'space'), may hold values from 0 to 511, as said below
- conv_first: bfloat16 [27, 256, 256], replicated, may hold values from -0.078125 to 0.078125
- conv_second: bfloat16 [27, 256, 256], replicated, may hold values from -0.078125 to 0.078125
- gain_first: float32 [256], replicated, may hold values from 0.1 to 1.9
- gain_second: float32 [256], replicated, may hold values from 0.1 to 1.9
- down_weight: bfloat16 [256, 512], replicated, may hold values from -0.375 to 0.375
- cotangent: bfloat16 [4, 512, 512], P('dp', 'space'), may hold values from -6 to 6
Outputs:
- fine_out: bfloat16 [4, 2048, 256], P('dp', 'space')
- coarse: bfloat16 [4, 512, 512], P('dp', 'space')
- down_grad: float32 [256, 512], replicated
Inputs may be any that keep to these rules, and one draw needn't show every extreme that they name: `neighbours`: for a site s of the block [d * 256, (d + 1) * 256), every entry is -1 or lies in [(d - 1) * 256, (d + 2) * 256); entry 13 is s itself. The parents of the sites of the block [d * 256, (d + 1) * 256) never decrease along the block and lie in [d * 64, (d + 2) * 64).
All inputs are finite; a program needn't handle non-finite values.
Results may differ from a plain program's by a relative error of at most 0.0057.
Values may be sent and summed in bfloat16 or wider, within the bound.
A program may use at most 64 MiB of HBM per device.

v0:
```python
import math
import jax
import jax.numpy as jnp
from jax import lax
from jax.sharding import PartitionSpec as P


def extended(cells, sides, width):
    for axis, dim in sides:
        count = lax.axis_size(axis)
        ends = count - 1
        head = lax.slice_in_dim(cells, 0, width, axis=dim)
        tail = lax.slice_in_dim(cells, cells.shape[dim] - width, cells.shape[dim], axis=dim)
        cells = jnp.concatenate(
            [
                lax.ppermute(tail, axis, [(i, (i + 1) % count) for i in range(ends)]),
                cells,
                lax.ppermute(head, axis, [((i + 1) % count, i) for i in range(ends)]),
            ],
            axis=dim,
        )
    return cells


def from_behind(array, axis, by):
    length = lax.axis_size(axis)
    pairs = [(i, i + by) for i in range(length) if 0 <= i + by < length]
    return lax.ppermute(array, axis, pairs)


def convolve(field, tap_lists, weights):
    site_rows = field.shape[1]
    nearby = extended(field, (("space", 1),), site_rows)
    lowest = (lax.axis_index("space") - 1) * site_rows
    lookup = jnp.where(tap_lists < 0, 3 * site_rows, tap_lists - lowest)
    window_ids = jnp.arange(3 * site_rows, dtype=jnp.int32)

    def one_tap(running, inputs):
        rows_now, weight = inputs
        selector = (rows_now[:, :, None] == window_ids[None, None, :]).astype(jnp.bfloat16)
        picked = jnp.einsum(
            "wsr,wrc->wsc", selector, nearby, preferred_element_type=jnp.float32
        ).astype(jnp.bfloat16)
        return (
            running + jnp.einsum("wsc,cd->wsd", picked, weight, preferred_element_type=jnp.float32),
            None,
        )

    start = jnp.zeros((field.shape[0], site_rows, weights.shape[2]), jnp.float32)
    running, _ = lax.scan(one_tap, start, (jnp.moveaxis(lookup, 1, 0), weights))
    return running


def settle(running, gain):
    inverse = lax.rsqrt(jnp.mean(running * running, axis=-1, keepdims=True) + 1e-05)
    return jax.nn.silu(running * inverse * gain)


def body(
    features,
    neighbours,
    parents,
    conv_first,
    conv_second,
    gain_first,
    gain_second,
    down_weight,
    cotangent,
):
    middle = settle(convolve(features, neighbours, conv_first), gain_first).astype(jnp.bfloat16)
    fine_out = (
        features.astype(jnp.float32)
        + settle(convolve(middle, neighbours, conv_second), gain_second)
    ).astype(jnp.bfloat16)
    par_rows = cotangent.shape[1]
    owner_id = lax.axis_index("space")
    world_rows = features.shape[0]
    parent_ids = owner_id * par_rows + jnp.arange(2 * par_rows, dtype=jnp.int32)
    onehot = (parents[:, None, :] == parent_ids[None, :, None]).astype(jnp.bfloat16)
    partial_value = jnp.einsum("wps,wsc->wpc", onehot, fine_out, preferred_element_type=jnp.float32)
    tallies = jnp.sum(onehot.astype(jnp.float32), axis=2)
    moved = from_behind((partial_value[:, par_rows:], tallies[:, par_rows:]), "space", 1)
    parent_sums = partial_value[:, :par_rows] + moved[0]
    counts = tallies[:, :par_rows] + moved[1]
    pooled = (parent_sums / jnp.maximum(counts, 1.0)[:, :, None]).astype(jnp.bfloat16)
    coarse = jnp.einsum(
        "wpc,cd->wpd", pooled, down_weight, preferred_element_type=jnp.float32
    ).astype(jnp.bfloat16)
    local_grad = jnp.einsum("wpc,wpd->cd", pooled, cotangent, preferred_element_type=jnp.float32)
    worlds_all = world_rows * lax.axis_size("dp")
    parents_all = par_rows * lax.axis_size("space")
    down_grad = lax.psum(local_grad, ("dp", "space")) * (1.0 / math.sqrt(worlds_all * parents_all))
    return (fine_out, coarse, down_grad)


def solution(mesh):
    return jax.shard_map(
        body,
        mesh=mesh,
        in_specs=(
            P("dp", "space", None),
            P("dp", None, "space"),
            P("dp", "space"),
            P(),
            P(),
            P(),
            P(),
            P(),
            P("dp", "space", None),
        ),
        out_specs=(P("dp", "space", None), P("dp", "space", None), P()),
        check_vma=False,
    )
```

profile of v0, /device:TPU:0, one launch (start us, length us, event | category | flops | bytes accessed | tf_op | source)
XLA Modules:
  0.0 252.0 jit_solution(10413457237684646482)
XLA Ops:
  7.2 2.5 %collective-permute-start = (bf16[1,256,256]{2,1,0:T(8,128)(2,1)}, bf16[1,256,256]{2,1,0:T(8,128)(2,1)S(1)}, u32[]{:S(2)}, u32[]{:S(2)}) collective-permute-start(bf16[1,256,256]{2,1,0:T(8,128)(2,1)} %param.13), channel_id=1, source_target_pairs={{0,1},{1,2},{2,3},{3,4},{4,5},{5,6},{6,7},{8,9},{9,10},{10,11},{11... | collective-permute-start | bytes 393224 | tf_op jit(solution)/shard_map/ppermute | solution.py:16
  9.8 1.3 collective-permute-start.1
  11.9 3.5 %collective-permute-done.1 = bf16[1,256,256]{2,1,0:T(8,128)(2,1)S(1)} collective-permute-done((bf16[1,256,256]{2,1,0:T(8,128)(2,1)}, bf16[1,256,256]{2,1,0:T(8,128)(2,1)S(1)}, u32[]{:S(2)}, u32[]{:S(2)}) %collective-permute-start.1) | collective-permute-done | bytes 131104 | tf_op jit(solution)/shard_map/ppermute | solution.py:18
  16.4 39.3 %while.22 = (s32[]{:T(128)}, f32[1,256,256]{2,1,0:T(8,128)S(1)}, s32[27,1,256]{2,1,0:T(1,128)S(1)}, bf16[1,768,256]{2,1,0:T(8,128)(2,1)S(1)}, bf16[27,256,256]{2,1,0:T(8,128)(2,1)}, /*index=5*/s32[]{:T(128)}, s32[]{:T(128)}) while((s32[]{:T(128)}, f32[1,256,256]{2,1,0:T(8,128)S(1)}, s32[27,1,256]{2,1,0:T(1,128)S(1)}, ...), condition=%wide.region_1.2_spmd.clone, body=%wide.region_0.1_spmd.clone.sunk | while | flops 134610944 | bytes 1052251 | solution.py:50
  16.4 1.4 fusion.50
  17.8 1.4 fusion.50
  19.3 1.4 fusion.50
  20.8 1.4 fusion.50
  22.2 1.4 fusion.50
  23.7 1.4 fusion.50
  25.1 1.4 fusion.50
  26.6 1.4 fusion.50
  28.0 1.4 fusion.50
  29.5 1.4 fusion.50
  31.0 1.4 fusion.50
  32.4 1.4 fusion.50
  33.9 1.4 fusion.50
  35.3 1.4 fusion.50
  36.8 1.4 fusion.50
  38.2 1.4 fusion.50
  39.7 1.4 fusion.50
  41.2 1.4 fusion.50
  42.6 1.4 fusion.50
  44.1 1.4 fusion.50
  45.5 1.4 fusion.50
  47.0 1.4 fusion.50
  48.4 1.4 fusion.50
  49.9 1.4 fusion.50
  51.3 1.4 fusion.50
  52.8 1.4 fusion.50
  54.3 1.4 fusion.50
  56.0 5.5 %collective-permute-start.2 = (bf16[1,256,256]{2,1,0:T(8,128)(2,1)S(1)}, bf16[1,256,256]{2,1,0:T(8,128)(2,1)S(1)}, u32[]{:S(2)}, u32[]{:S(2)}) collective-permute-start(bf16[1,256,256]{2,1,0:T(8,128)(2,1)S(1)} %multiply_convert_fusion), channel_id=1, source_target_pairs={{0,1},{1,2},{2,3},{3,4},{4,5},{5,6},{6,7},{8,9},{9,10},{10,11},{11... | collective-permute-start | bytes 393224 | tf_op jit(solution)/shard_map/ppermute | solution.py:16
  63.0 3.0 %collective-permute-start.5 = (f32[1,64]{1,0:T(1,128)S(1)}, f32[1,64]{1,0:T(1,128)S(1)}, u32[]{:S(2)}, u32[]{:S(2)}) collective-permute-start(f32[1,64]{1,0:T(1,128)S(1)} %slice.15), channel_id=1, source_target_pairs={{0,1},{1,2},{2,3},{3,4},{4,5},{5,6},{6,7},{8,9},{9,10},{10,11},{11... | collective-permute-start | bytes 776 | tf_op jit(solution)/shard_map/ppermute | solution.py:28
  66.2 39.3 %while.23 = (s32[]{:T(128)}, f32[1,256,256]{2,1,0:T(8,128)S(1)}, s32[27,1,256]{2,1,0:T(1,128)S(1)}, bf16[1,768,256]{2,1,0:T(8,128)(2,1)S(1)}, bf16[27,256,256]{2,1,0:T(8,128)(2,1)}, /*index=5*/s32[]{:T(128)}, s32[]{:T(128)}) while((s32[]{:T(128)}, f32[1,256,256]{2,1,0:T(8,128)S(1)}, s32[27,1,256]{2,1,0:T(1,128)S(1)}, ...), condition=%wide.region_4.5_spmd.clone, body=%wide.region_3.4_spmd.clone.sunk | while | flops 134610944 | bytes 1052251 | solution.py:50
  66.2 1.4 fusion.54
  67.7 1.4 fusion.54
  69.1 1.4 fusion.54
  70.6 1.4 fusion.54
  72.0 1.4 fusion.54
  73.5 1.4 fusion.54
  74.9 1.4 fusion.54
  76.4 1.4 fusion.54
  77.9 1.4 fusion.54
  79.3 1.4 fusion.54
  80.8 1.4 fusion.54
  82.2 1.4 fusion.54
  83.7 1.4 fusion.54
  85.1 1.4 fusion.54
  86.6 1.4 fusion.54
  88.1 1.4 fusion.54
  89.5 1.4 fusion.54
  91.0 1.4 fusion.54
  92.4 1.4 fusion.54
  93.9 1.4 fusion.54
  95.3 1.4 fusion.54
  96.8 1.4 fusion.54
  98.3 1.4 fusion.54
  99.7 1.4 fusion.54
  101.2 1.4 fusion.54
  102.6 1.4 fusion.54
  104.1 1.4 fusion.54
  106.1 3.6 %collective-permute-start.4 = (f32[1,64,256]{2,1,0:T(8,128)S(1)}, f32[1,64,256]{2,1,0:T(8,128)S(1)}, u32[]{:S(2)}, u32[]{:S(2)}) collective-permute-start(f32[1,64,256]{2,1,0:T(8,128)S(1)} %slice.17), channel_id=1, source_target_pairs={{0,1},{1,2},{2,3},{3,4},{4,5},{5,6},{6,7},{8,9},{9,10},{10,11},{11... | collective-permute-start | bytes 196616 | tf_op jit(solution)/shard_map/ppermute | solution.py:28
  112.5 130.8 %all-reduce.2.cloned.1.call-done = f32[256,512]{1,0:T(8,128)} async-done(((f32[256,512]{1,0:T(8,128)}), f32[256,512]{1,0:T(8,128)}) %all-reduce.2.cloned.1.call-update) | async-done | bytes 524304 | tf_op jit(solution)/shard_map/psum | solution.py:92
  243.2 1.9 broadcast_multiply_fusion
  (96 shorter events, 7.3 us)
Async XLA Ops:
  7.2 104.5 %copy-start = (bf16[256,512]{1,0:T(8,128)(2,1)S(1)}, bf16[256,512]{1,0:T(8,128)(2,1)}, u32[]{:S(2)}) copy-start(bf16[256,512]{1,0:T(8,128)(2,1)} %param.20) | copy-start | bytes 786436
  7.2 48.7 %copy-start.5 = (f32[256]{0:T(256)S(1)}, f32[256]{0:T(256)}, u32[]{:S(2)}) copy-start(f32[256]{0:T(256)} %param.18) | copy-start | bytes 3076
  7.2 55.6 %copy-start.4 = (s32[1,256]{1,0:T(1,128)S(1)}, s32[1,256]{1,0:T(1,128)}, u32[]{:S(2)}) copy-start(s32[1,256]{1,0:T(1,128)} %param.15) | copy-start | bytes 3076
  7.2 236.0 %all-reduce.2.cloned.1.call-start = ((), (), s32[]{:S(2)}) async-start(), calls=%async_computation | async-start | bytes 1048576 | tf_op jit(solution)/shard_map/psum | solution.py:92
  7.2 4.6 %collective-permute-start = (bf16[1,256,256]{2,1,0:T(8,128)(2,1)}, bf16[1,256,256]{2,1,0:T(8,128)(2,1)S(1)}, u32[]{:S(2)}, u32[]{:S(2)}) collective-permute-start(bf16[1,256,256]{2,1,0:T(8,128)(2,1)} %param.13), channel_id=1, source_target_pairs={{0,1},{1,2},{2,3},{3,4},{4,5},{5,6},{6,7},{8,9},{9,10},{10,11},{11... | collective-permute-start | bytes 393224 | tf_op jit(solution)/shard_map/ppermute | solution.py:16
  9.8 5.6 %collective-permute-start.1 = (bf16[1,256,256]{2,1,0:T(8,128)(2,1)}, bf16[1,256,256]{2,1,0:T(8,128)(2,1)S(1)}, u32[]{:S(2)}, u32[]{:S(2)}) collective-permute-start(bf16[1,256,256]{2,1,0:T(8,128)(2,1)} %param.13), channel_id=1, source_target_pairs={{1,0},{2,1},{3,2},{4,3},{5,4},{6,5},{7,6},{9,8},{10,9},{11,10},{12... | collective-permute-start | bytes 393224 | tf_op jit(solution)/shard_map/ppermute | solution.py:18
  55.7 50.0 %copy-start.2 = (bf16[1,256,256]{2,1,0:T(8,128)(2,1)S(1)}, bf16[1,256,256]{2,1,0:T(8,128)(2,1)}, u32[]{:S(2)}) copy-start(bf16[1,256,256]{2,1,0:T(8,128)(2,1)} %param.13) | copy-start | bytes 393220
  55.7 49.9 %copy-start.6 = (f32[256]{0:T(256)S(1)}, f32[256]{0:T(256)}, u32[]{:S(2)}) copy-start(f32[256]{0:T(256)} %param.19) | copy-start | bytes 3076
  56.0 10.1 %collective-permute-start.2 = (bf16[1,256,256]{2,1,0:T(8,128)(2,1)S(1)}, bf16[1,256,256]{2,1,0:T(8,128)(2,1)S(1)}, u32[]{:S(2)}, u32[]{:S(2)}) collective-permute-start(bf16[1,256,256]{2,1,0:T(8,128)(2,1)S(1)} %multiply_convert_fusion), channel_id=1, source_target_pairs={{0,1},{1,2},{2,3},{3,4},{4,5},{5,6},{6,7},{8,9},{9,10},{10,11},{11... | collective-permute-start | bytes 393224 | tf_op jit(solution)/shard_map/ppermute | solution.py:16
  61.5 4.6 %collective-permute-start.3 = (bf16[1,256,256]{2,1,0:T(8,128)(2,1)S(1)}, bf16[1,256,256]{2,1,0:T(8,128)(2,1)S(1)}, u32[]{:S(2)}, u32[]{:S(2)}) collective-permute-start(bf16[1,256,256]{2,1,0:T(8,128)(2,1)S(1)} %multiply_convert_fusion), channel_id=1, source_target_pairs={{1,0},{2,1},{3,2},{4,3},{5,4},{6,5},{7,6},{9,8},{10,9},{11,10},{12... | collective-permute-start | bytes 393224 | tf_op jit(solution)/shard_map/ppermute | solution.py:18
  63.0 46.6 %collective-permute-start.5 = (f32[1,64]{1,0:T(1,128)S(1)}, f32[1,64]{1,0:T(1,128)S(1)}, u32[]{:S(2)}, u32[]{:S(2)}) collective-permute-start(f32[1,64]{1,0:T(1,128)S(1)} %slice.15), channel_id=1, source_target_pairs={{0,1},{1,2},{2,3},{3,4},{4,5},{5,6},{6,7},{8,9},{9,10},{10,11},{11... | collective-permute-start | bytes 776 | tf_op jit(solution)/shard_map/ppermute | solution.py:28
  66.2 44.4 %copy-start.3 = (bf16[1,64,512]{2,1,0:T(8,128)(2,1)S(1)}, bf16[1,64,512]{2,1,0:T(8,128)(2,1)}, u32[]{:S(2)}) copy-start(bf16[1,64,512]{2,1,0:T(8,128)(2,1)} %param.21) | copy-start | bytes 196612
  105.8 139.3 %copy-start.1 = (bf16[1,256,256]{2,1,0:T(8,128)(2,1)}, bf16[1,256,256]{2,1,0:T(8,128)(2,1)S(1)}, u32[]{:S(2)}) copy-start(bf16[1,256,256]{2,1,0:T(8,128)(2,1)S(1)} %add_convert_fusion) | copy-start | bytes 393220
  106.1 4.4 %collective-permute-start.4 = (f32[1,64,256]{2,1,0:T(8,128)S(1)}, f32[1,64,256]{2,1,0:T(8,128)S(1)}, u32[]{:S(2)}, u32[]{:S(2)}) collective-permute-start(f32[1,64,256]{2,1,0:T(8,128)S(1)} %slice.17), channel_id=1, source_target_pairs={{0,1},{1,2},{2,3},{3,4},{4,5},{5,6},{6,7},{8,9},{9,10},{10,11},{11... | collective-permute-start | bytes 196616 | tf_op jit(solution)/shard_map/ppermute | solution.py:28
Sparse Core Ops, SparseCore 0:
  111.8 131.4 all-reduce.1
where the time goes:
time: 253 us; the launch traced here: 252 us
  waiting for transfers between devices  135 us (53%)
  matrix products  78.4 us (31%)
  starting transfers between devices  17.2 us (7%)
  between operations  14.3 us (6%)
  other arithmetic  4.43 us (2%)
    psum x1, waiting for transfers between devices, body(): lax.psum(local_grad, ('dp', 'space'))  131 us
    dot_general x54, matrix products, one_tap(): jnp.einsum('wsc,cd->wsd', picked, weight, preferred_element_type=jnp.floa...  76.4 us
    ppermute x2, starting transfers between devices, extended(): lax.ppermute(tail, axis, [(i, (i + 1) % count) for i in range(ends)])  8 us
    ppermute x2, starting transfers between devices, from_behind(): return lax.ppermute(array, axis, pairs)  6.59 us
  transfers between devices with their start and end apart: 7, of which 3 were waited for; matrix products, arithmetic and copies ran while one was open for 16% of the time, Pallas kernels for 0%

commit v1 on v0

--- a/solution.py
+++ b/solution.py
@@ -89,7 +89,9 @@
     local_grad = jnp.einsum("wpc,wpd->cd", pooled, cotangent, preferred_element_type=jnp.float32)
     worlds_all = world_rows * lax.axis_size("dp")
     parents_all = par_rows * lax.axis_size("space")
-    down_grad = lax.psum(local_grad, ("dp", "space")) * (1.0 / math.sqrt(worlds_all * parents_all))
+    down_grad = jnp.sum(lax.all_gather(local_grad, ("dp", "space")), axis=0) * (
+        1.0 / math.sqrt(worlds_all * parents_all)
+    )
     return (fine_out, coarse, down_grad)
 
 

time: 253 us -> 245 us (0.968)
  waiting for transfers between devices: 135 us -> 120 us
  other arithmetic: 4.43 us -> 11.1 us
    psum x1 -> x0, waiting for transfers between devices: 131 us -> none  [body(): lax.psum(local_grad, ('dp', 'space'))]
    all_gather x0 -> x1, waiting for transfers between devices: none -> 116 us  [body(): lax.all_gather(local_grad, ('dp', 'space'))]
    reduce_sum x0 -> x1, other arithmetic: none -> 7.75 us  [body(): jnp.sum(lax.all_gather(local_grad, ('dp', 'space')), axis=0)]
  transfers between devices with their start and end apart: 7 -> 7, of which waited for: 3 -> 3; matrix products, arithmetic and copies ran while one was open for 16% -> 17% of each run, Pallas kernels for 0% -> 0%
where the time goes in v1:
time: 245 us; the launch traced here: 244 us
  waiting for transfers between devices  120 us (49%)
  matrix products  78.4 us (32%)
  starting transfers between devices  17.2 us (7%)
  between operations  14.3 us (6%)
  other arithmetic  11.1 us (5%)
    all_gather x1, waiting for transfers between devices, body(): lax.all_gather(local_grad, ('dp', 'space'))  116 us
    dot_general x54, matrix products, one_tap(): jnp.einsum('wsc,cd->wsd', picked, weight, preferred_element_type=jnp.floa...  76.4 us
    ppermute x2, starting transfers between devices, extended(): lax.ppermute(tail, axis, [(i, (i + 1) % count) for i in range(ends)])  8 us
    reduce_sum x1, other arithmetic, body(): jnp.sum(lax.all_gather(local_grad, ('dp', 'space')), axis=0)  7.75 us
    ppermute x2, starting transfers between devices, from_behind(): return lax.ppermute(array, axis, pairs)  6.59 us
  transfers between devices with their start and end apart: 7, of which 3 were waited for; matrix products, arithmetic and copies ran while one was open for 17% of the time, Pallas kernels for 0%

profile of v1, /device:TPU:0, one launch (start us, length us, event | category | flops | bytes accessed | tf_op | source)
XLA Modules:
  0.0 244.0 jit_solution(2095348619847725217)
XLA Ops:
  7.2 2.5 %collective-permute-start = (bf16[1,256,256]{2,1,0:T(8,128)(2,1)}, bf16[1,256,256]{2,1,0:T(8,128)(2,1)S(1)}, u32[]{:S(2)}, u32[]{:S(2)}) collective-permute-start(bf16[1,256,256]{2,1,0:T(8,128)(2,1)} %param.13), channel_id=1, source_target_pairs={{0,1},{1,2},{2,3},{3,4},{4,5},{5,6},{6,7},{8,9},{9,10},{10,11},{11... | collective-permute-start | bytes 393224 | tf_op jit(solution)/shard_map/ppermute | solution.py:16
  9.8 1.3 collective-permute-start.1
  11.9 3.5 %collective-permute-done.1 = bf16[1,256,256]{2,1,0:T(8,128)(2,1)S(1)} collective-permute-done((bf16[1,256,256]{2,1,0:T(8,128)(2,1)}, bf16[1,256,256]{2,1,0:T(8,128)(2,1)S(1)}, u32[]{:S(2)}, u32[]{:S(2)}) %collective-permute-start.1) | collective-permute-done | bytes 131104 | tf_op jit(solution)/shard_map/ppermute | solution.py:18
  16.4 39.3 %while.22 = (s32[]{:T(128)}, f32[1,256,256]{2,1,0:T(8,128)S(1)}, s32[27,1,256]{2,1,0:T(1,128)S(1)}, bf16[1,768,256]{2,1,0:T(8,128)(2,1)S(1)}, bf16[27,256,256]{2,1,0:T(8,128)(2,1)}, /*index=5*/s32[]{:T(128)}, s32[]{:T(128)}) while((s32[]{:T(128)}, f32[1,256,256]{2,1,0:T(8,128)S(1)}, s32[27,1,256]{2,1,0:T(1,128)S(1)}, ...), condition=%wide.region_1.2_spmd.clone, body=%wide.region_0.1_spmd.clone.sunk | while | flops 134610944 | bytes 1052251 | solution.py:50
  16.4 1.4 fusion.50
  17.8 1.4 fusion.50
  19.3 1.4 fusion.50
  20.8 1.4 fusion.50
  22.2 1.4 fusion.50
  23.7 1.4 fusion.50
  25.1 1.4 fusion.50
  26.6 1.4 fusion.50
  28.0 1.4 fusion.50
  29.5 1.4 fusion.50
  31.0 1.4 fusion.50
  32.4 1.4 fusion.50
  33.9 1.4 fusion.50
  35.3 1.4 fusion.50
  36.8 1.4 fusion.50
  38.2 1.4 fusion.50
  39.7 1.4 fusion.50
  41.2 1.4 fusion.50
  42.6 1.4 fusion.50
  44.1 1.4 fusion.50
  45.5 1.4 fusion.50
  47.0 1.4 fusion.50
  48.4 1.4 fusion.50
  49.9 1.4 fusion.50
  51.3 1.4 fusion.50
  52.8 1.4 fusion.50
  54.3 1.4 fusion.50
  56.0 5.5 %collective-permute-start.2 = (bf16[1,256,256]{2,1,0:T(8,128)(2,1)S(1)}, bf16[1,256,256]{2,1,0:T(8,128)(2,1)S(1)}, u32[]{:S(2)}, u32[]{:S(2)}) collective-permute-start(bf16[1,256,256]{2,1,0:T(8,128)(2,1)S(1)} %multiply_convert_fusion), channel_id=1, source_target_pairs={{0,1},{1,2},{2,3},{3,4},{4,5},{5,6},{6,7},{8,9},{9,10},{10,11},{11... | collective-permute-start | bytes 393224 | tf_op jit(solution)/shard_map/ppermute | solution.py:16
  63.0 3.0 %collective-permute-start.5 = (f32[1,64]{1,0:T(1,128)S(1)}, f32[1,64]{1,0:T(1,128)S(1)}, u32[]{:S(2)}, u32[]{:S(2)}) collective-permute-start(f32[1,64]{1,0:T(1,128)S(1)} %slice.15), channel_id=1, source_target_pairs={{0,1},{1,2},{2,3},{3,4},{4,5},{5,6},{6,7},{8,9},{9,10},{10,11},{11... | collective-permute-start | bytes 776 | tf_op jit(solution)/shard_map/ppermute | solution.py:28
  66.2 39.3 %while.23 = (s32[]{:T(128)}, f32[1,256,256]{2,1,0:T(8,128)S(1)}, s32[27,1,256]{2,1,0:T(1,128)S(1)}, bf16[1,768,256]{2,1,0:T(8,128)(2,1)S(1)}, bf16[27,256,256]{2,1,0:T(8,128)(2,1)}, /*index=5*/s32[]{:T(128)}, s32[]{:T(128)}) while((s32[]{:T(128)}, f32[1,256,256]{2,1,0:T(8,128)S(1)}, s32[27,1,256]{2,1,0:T(1,128)S(1)}, ...), condition=%wide.region_4.5_spmd.clone, body=%wide.region_3.4_spmd.clone.sunk | while | flops 134610944 | bytes 1052251 | solution.py:50
  66.2 1.4 fusion.54
  67.7 1.4 fusion.54
  69.1 1.4 fusion.54
  70.6 1.4 fusion.54
  72.0 1.4 fusion.54
  73.5 1.4 fusion.54
  74.9 1.4 fusion.54
  76.4 1.4 fusion.54
  77.9 1.4 fusion.54
  79.3 1.4 fusion.54
  80.8 1.4 fusion.54
  82.2 1.4 fusion.54
  83.7 1.4 fusion.54
  85.1 1.4 fusion.54
  86.6 1.4 fusion.54
  88.1 1.4 fusion.54
  89.5 1.4 fusion.54
  91.0 1.4 fusion.54
  92.4 1.4 fusion.54
  93.9 1.4 fusion.54
  95.3 1.4 fusion.54
  96.8 1.4 fusion.54
  98.3 1.4 fusion.54
  99.7 1.4 fusion.54
  101.2 1.4 fusion.54
  102.6 1.4 fusion.54
  104.1 1.4 fusion.54
  106.1 3.6 %collective-permute-start.4 = (f32[1,64,256]{2,1,0:T(8,128)S(1)}, f32[1,64,256]{2,1,0:T(8,128)S(1)}, u32[]{:S(2)}, u32[]{:S(2)}) collective-permute-start(f32[1,64,256]{2,1,0:T(8,128)S(1)} %slice.17), channel_id=1, source_target_pairs={{0,1},{1,2},{2,3},{3,4},{4,5},{5,6},{6,7},{8,9},{9,10},{10,11},{11... | collective-permute-start | bytes 196616 | tf_op jit(solution)/shard_map/ppermute | solution.py:28
  112.5 116.1 %all-gather.3.cloned.1.call-done = f32[8192,512]{1,0:T(8,128)} async-done(((f32[256,512]{1,0:T(8,128)}), f32[8192,512]{1,0:T(8,128)}) %all-gather.3.cloned.1.call-update) | async-done | bytes 16777232 | tf_op jit(solution)/shard_map/all_gather | solution.py:92
  228.6 7.8 %reduce_sum.42 = f32[256,512]{1,0:T(8,128)S(1)} reduce(f32[32,256,512]{2,1,0:T(8,128)} %bitcast.75, f32[]{:T(128)} %constant.24.clone.1), dimensions={0}, to_apply=%region_7.8 | reduce | flops 4063232 | bytes 17301508 | tf_op jit(solution)/shard_map/reduce_sum | solution.py:92
  (97 shorter events, 8.2 us)
Async XLA Ops:
  7.2 104.5 %copy-start = (bf16[256,512]{1,0:T(8,128)(2,1)S(1)}, bf16[256,512]{1,0:T(8,128)(2,1)}, u32[]{:S(2)}) copy-start(bf16[256,512]{1,0:T(8,128)(2,1)} %param.20) | copy-start | bytes 786436
  7.2 48.7 %copy-start.5 = (f32[256]{0:T(256)S(1)}, f32[256]{0:T(256)}, u32[]{:S(2)}) copy-start(f32[256]{0:T(256)} %param.18) | copy-start | bytes 3076
  7.2 55.6 %copy-start.4 = (s32[1,256]{1,0:T(1,128)S(1)}, s32[1,256]{1,0:T(1,128)}, u32[]{:S(2)}) copy-start(s32[1,256]{1,0:T(1,128)} %param.15) | copy-start | bytes 3076
  7.2 221.4 %all-gather.3.cloned.1.call-start = ((), (), s32[]{:S(2)}) async-start(), calls=%async_computation | async-start | bytes 17301504 | tf_op jit(solution)/shard_map/all_gather | solution.py:92
  7.2 4.6 %collective-permute-start = (bf16[1,256,256]{2,1,0:T(8,128)(2,1)}, bf16[1,256,256]{2,1,0:T(8,128)(2,1)S(1)}, u32[]{:S(2)}, u32[]{:S(2)}) collective-permute-start(bf16[1,256,256]{2,1,0:T(8,128)(2,1)} %param.13), channel_id=1, source_target_pairs={{0,1},{1,2},{2,3},{3,4},{4,5},{5,6},{6,7},{8,9},{9,10},{10,11},{11... | collective-permute-start | bytes 393224 | tf_op jit(solution)/shard_map/ppermute | solution.py:16
  9.8 5.6 %collective-permute-start.1 = (bf16[1,256,256]{2,1,0:T(8,128)(2,1)}, bf16[1,256,256]{2,1,0:T(8,128)(2,1)S(1)}, u32[]{:S(2)}, u32[]{:S(2)}) collective-permute-start(bf16[1,256,256]{2,1,0:T(8,128)(2,1)} %param.13), channel_id=1, source_target_pairs={{1,0},{2,1},{3,2},{4,3},{5,4},{6,5},{7,6},{9,8},{10,9},{11,10},{12... | collective-permute-start | bytes 393224 | tf_op jit(solution)/shard_map/ppermute | solution.py:18
  55.7 50.0 %copy-start.2 = (bf16[1,256,256]{2,1,0:T(8,128)(2,1)S(1)}, bf16[1,256,256]{2,1,0:T(8,128)(2,1)}, u32[]{:S(2)}) copy-start(bf16[1,256,256]{2,1,0:T(8,128)(2,1)} %param.13) | copy-start | bytes 393220
  55.7 49.9 %copy-start.6 = (f32[256]{0:T(256)S(1)}, f32[256]{0:T(256)}, u32[]{:S(2)}) copy-start(f32[256]{0:T(256)} %param.19) | copy-start | bytes 3076
  56.0 10.1 %collective-permute-start.2 = (bf16[1,256,256]{2,1,0:T(8,128)(2,1)S(1)}, bf16[1,256,256]{2,1,0:T(8,128)(2,1)S(1)}, u32[]{:S(2)}, u32[]{:S(2)}) collective-permute-start(bf16[1,256,256]{2,1,0:T(8,128)(2,1)S(1)} %multiply_convert_fusion), channel_id=1, source_target_pairs={{0,1},{1,2},{2,3},{3,4},{4,5},{5,6},{6,7},{8,9},{9,10},{10,11},{11... | collective-permute-start | bytes 393224 | tf_op jit(solution)/shard_map/ppermute | solution.py:16
  61.5 4.6 %collective-permute-start.3 = (bf16[1,256,256]{2,1,0:T(8,128)(2,1)S(1)}, bf16[1,256,256]{2,1,0:T(8,128)(2,1)S(1)}, u32[]{:S(2)}, u32[]{:S(2)}) collective-permute-start(bf16[1,256,256]{2,1,0:T(8,128)(2,1)S(1)} %multiply_convert_fusion), channel_id=1, source_target_pairs={{1,0},{2,1},{3,2},{4,3},{5,4},{6,5},{7,6},{9,8},{10,9},{11,10},{12... | collective-permute-start | bytes 393224 | tf_op jit(solution)/shard_map/ppermute | solution.py:18
  63.0 46.6 %collective-permute-start.5 = (f32[1,64]{1,0:T(1,128)S(1)}, f32[1,64]{1,0:T(1,128)S(1)}, u32[]{:S(2)}, u32[]{:S(2)}) collective-permute-start(f32[1,64]{1,0:T(1,128)S(1)} %slice.15), channel_id=1, source_target_pairs={{0,1},{1,2},{2,3},{3,4},{4,5},{5,6},{6,7},{8,9},{9,10},{10,11},{11... | collective-permute-start | bytes 776 | tf_op jit(solution)/shard_map/ppermute | solution.py:28
  66.2 44.4 %copy-start.3 = (bf16[1,64,512]{2,1,0:T(8,128)(2,1)S(1)}, bf16[1,64,512]{2,1,0:T(8,128)(2,1)}, u32[]{:S(2)}) copy-start(bf16[1,64,512]{2,1,0:T(8,128)(2,1)} %param.21) | copy-start | bytes 196612
  105.8 130.5 %copy-start.1 = (bf16[1,256,256]{2,1,0:T(8,128)(2,1)}, bf16[1,256,256]{2,1,0:T(8,128)(2,1)S(1)}, u32[]{:S(2)}) copy-start(bf16[1,256,256]{2,1,0:T(8,128)(2,1)S(1)} %add_convert_fusion) | copy-start | bytes 393220
  106.1 4.4 %collective-permute-start.4 = (f32[1,64,256]{2,1,0:T(8,128)S(1)}, f32[1,64,256]{2,1,0:T(8,128)S(1)}, u32[]{:S(2)}, u32[]{:S(2)}) collective-permute-start(f32[1,64,256]{2,1,0:T(8,128)S(1)} %slice.17), channel_id=1, source_target_pairs={{0,1},{1,2},{2,3},{3,4},{4,5},{5,6},{6,7},{8,9},{9,10},{10,11},{11... | collective-permute-start | bytes 196616 | tf_op jit(solution)/shard_map/ppermute | solution.py:28
Sparse Core Ops, SparseCore 0:
  111.8 116.7 all-gather.2
